TPU v7x, 32 devices: a whole 2x2x4 slice. The times are simulated.
32 devices in a mesh: rows: 2 (over y), seq: 16 (over z, x, core).
Axes of the slice: x: 2, y: 2, z: 4, core: 2. Of those that a mesh axis runs over, the one named last changes fastest.
Arguments:
- tokens: bfloat16 [2, 2048, 2304], P('rows', 'seq'), may hold values from -6 to 6
- cotangent: bfloat16 [2, 2048, 2304], P('rows', 'seq'), may hold values from -6 to 6
- doc_ids: int32 [2, 2048], P('rows'), may hold values from 0 to 3, as said below
- bit_levels: int32 [7], replicated, may hold values from 0 to 2, as said below
- w_query: int32 [2304, 2048], P(('rows', 'seq')), may hold values from -128 to 127
- w_key: int32 [2304, 1024], P(('rows', 'seq')), may hold values from -128 to 127
- w_value: int32 [2304, 1024], P(('rows', 'seq')), may hold values from -128 to 127
- w_proj: int32 [2304, 2048], P(('rows', 'seq')), may hold values from -128 to 127
- w_gate: int32 [2304, 9216], P(('rows', 'seq')), may hold values from -128 to 127
- w_up: int32 [2304, 9216], P(('rows', 'seq')), may hold values from -128 to 127
- w_down: int32 [2304, 9216], P(('rows', 'seq')), may hold values from -128 to 127
- gain_first: float32 [2304], replicated, may hold values from -0.5 to 0.5
- gain_second: float32 [2304], replicated, may hold values from -0.5 to 0.5
- gain_third: float32 [2304], replicated, may hold values from -0.5 to 0.5
- gain_fourth: float32 [2304], replicated, may hold values from -0.5 to 0.5
Outputs:
- layer_out: bfloat16 [2, 2048, 2304], P('rows', 'seq')
- grad_tokens: float32 [2, 2048, 2304], P('rows', 'seq')
- grad_query: float32 [2304, 2048], P(('rows', 'seq'))
- grad_key: float32 [2304, 1024], P(('rows', 'seq'))
- grad_value: float32 [2304, 1024], P(('rows', 'seq'))
- grad_proj: float32 [2304, 2048], P(('rows', 'seq'))
- grad_gate: float32 [2304, 9216], P(('rows', 'seq'))
- grad_up: float32 [2304, 9216], P(('rows', 'seq'))
- grad_down: float32 [2304, 9216], P(('rows', 'seq'))
- grad_first: float32 [2304], P(('rows', 'seq'))
- grad_second: float32 [2304], P(('rows', 'seq'))
- grad_third: float32 [2304], P(('rows', 'seq'))
- grad_fourth: float32 [2304], P(('rows', 'seq'))
Inputs may be any that keep to these rules, and one draw needn't show every extreme that they name: `doc_ids`: ids never fall along a row. Rows of even index hold one document (id 0); rows of odd index hold up to four, and their last token has id 3. `bit_levels`: level 0 occurs three times, levels 1 and 2 twice each.
All inputs are finite; a program needn't handle non-finite values.
Results may differ from a plain program's by a relative error of at most 0.019.
The roundings to bfloat16 on the way count: a program that leaves them out, or rounds other values in their place, can miss the bound.
Values may be sent and summed in bfloat16 or wider, within the bound.
A program may use at most 448 MiB of HBM per device.

v0:
```python
import math
import jax
import jax.numpy as jnp
from jax import lax
from jax.sharding import PartitionSpec as P

D = 2304
FF = 9216
HEADS = 8
KV_HEADS = 4
HEAD_DIM = 256
softcap = 50.0
epsilon = 1e-06
qk_boost = 1.65


def dequant(levels_int, level_idx, fan_in, boost):
    stride = jnp.where(level_idx == 0, 1, jnp.where(level_idx == 1, 16, 64)).astype(jnp.int32)
    sliced = levels_int // stride * stride + stride // 2
    return sliced.astype(jnp.float32) * (boost / (74.0 * math.sqrt(fan_in)))


def rmsnorm(values, gain_vec):
    return (
        values
        * lax.rsqrt(jnp.mean(values * values, axis=-1, keepdims=True) + epsilon)
        * (1.0 + gain_vec)
    )


def rotate(values, positions, direction):
    half_dim = HEAD_DIM // 2
    frequency = 10000.0 ** (-(2.0 / HEAD_DIM) * jnp.arange(half_dim, dtype=jnp.float32))
    angles = positions.astype(jnp.float32)[:, None] * frequency[None, :]
    cosine = jnp.cos(angles)[:, None, :]
    sine = jnp.sin(angles)[:, None, :] * direction
    front_half = values[..., :half_dim]
    back_half = values[..., half_dim:]
    return jnp.concatenate(
        [front_half * cosine - back_half * sine, back_half * cosine + front_half * sine], axis=-1
    )


def gelu_product(gate_vals, up_vals):
    return jax.nn.gelu(gate_vals, approximate=True) * up_vals


def per_device(
    tokens,
    cotangent,
    doc_ids,
    bit_levels,
    w_query,
    w_key,
    w_value,
    w_proj,
    w_gate,
    w_up,
    w_down,
    gain_first,
    gain_second,
    gain_third,
    gain_fourth,
):
    rows_here = tokens.shape[0]
    seq_block = tokens.shape[1]
    token_count = rows_here * seq_block
    local_rows = w_query.shape[0]
    group_size = HEADS // KV_HEADS
    query_width = HEADS * HEAD_DIM
    key_width = KV_HEADS * HEAD_DIM
    score_scale = HEAD_DIM ** (-0.5)
    offset = lax.axis_index("seq") * seq_block
    positions = offset + jnp.arange(seq_block, dtype=jnp.int32)
    query_docs = lax.dynamic_slice_in_dim(doc_ids, offset, seq_block, 1)
    query_local = dequant(w_query, bit_levels[0], D, qk_boost).astype(jnp.bfloat16)
    key_local = dequant(w_key, bit_levels[1], D, qk_boost).astype(jnp.bfloat16)
    value_local = dequant(w_value, bit_levels[2], D, 1.0).astype(jnp.bfloat16)
    proj_local = dequant(w_proj, bit_levels[3], query_width, 1.0).astype(jnp.bfloat16)
    gate_local = dequant(w_gate, bit_levels[4], D, 1.0).astype(jnp.bfloat16)
    up_local = dequant(w_up, bit_levels[5], D, 1.0).astype(jnp.bfloat16)
    down_local = dequant(w_down, bit_levels[6], FF, 1.0).astype(jnp.bfloat16)
    query_full, key_full, value_full, proj_full = (
        lax.all_gather(query_local, ("rows", "seq"), axis=0, tiled=True),
        lax.all_gather(key_local, ("rows", "seq"), axis=0, tiled=True),
        lax.all_gather(value_local, ("rows", "seq"), axis=0, tiled=True),
        lax.all_gather(proj_local, ("rows", "seq"), axis=0, tiled=True),
    )
    row_groups = lax.axis_size("rows")
    seq_count = lax.axis_size("seq")
    col_width = FF // seq_count
    stacked = jnp.stack([gate_local, up_local, down_local]).reshape(
        3, local_rows, seq_count, col_width
    )
    spread = jnp.concatenate([stacked] * row_groups, axis=2)
    columns_all = lax.all_to_all(
        spread, ("rows", "seq"), split_axis=2, concat_axis=1, tiled=True
    ).reshape(3, D, col_width)
    gate_cols = columns_all[0]
    up_cols = columns_all[1]
    down_cols = columns_all[2]
    flat_tokens = tokens.astype(jnp.float32).reshape(token_count, D)
    normed_low = rmsnorm(flat_tokens, gain_first).astype(jnp.bfloat16)
    query_pre = jnp.dot(normed_low, query_full, preferred_element_type=jnp.float32)
    key_pre = jnp.dot(normed_low, key_full, preferred_element_type=jnp.float32)
    value_low = (
        jnp.dot(normed_low, value_full, preferred_element_type=jnp.float32)
        .astype(jnp.bfloat16)
        .reshape(rows_here, seq_block, KV_HEADS, HEAD_DIM)
    )
    query_rot = (
        rotate(query_pre.reshape(rows_here, seq_block, HEADS, HEAD_DIM), positions, 1.0)
        .astype(jnp.bfloat16)
        .reshape(rows_here, seq_block, KV_HEADS, group_size, HEAD_DIM)
    )
    key_rot = rotate(
        key_pre.reshape(rows_here, seq_block, KV_HEADS, HEAD_DIM), positions, 1.0
    ).astype(jnp.bfloat16)

    def piece_weights(key_piece):
        key_count = key_piece.shape[1]
        key_pos = jnp.arange(key_count, dtype=jnp.int32)
        raw_scores = (
            jnp.einsum(
                "bqgrd,bkgd->bgrqk", query_rot, key_piece, preferred_element_type=jnp.float32
            )
            * score_scale
        )
        allowed = (key_pos[None, :] <= positions[:, None])[None] & (
            doc_ids[:, None, :] == query_docs[:, :, None]
        )
        bent_score = jnp.tanh(raw_scores / softcap)
        weights = jnp.where(allowed[:, None, None], jnp.exp(softcap * bent_score), 0.0)
        return (weights, bent_score)

    key_piece = lax.all_gather(key_rot, "seq", axis=1, tiled=True)
    value_piece = lax.all_gather(value_low, "seq", axis=1, tiled=True)
    weights, bent_score = piece_weights(key_piece)
    summed = jnp.einsum(
        "bgrqk,bkgd->bqgrd",
        weights.astype(jnp.bfloat16),
        value_piece,
        preferred_element_type=jnp.float32,
    )
    totals, summed = (jnp.sum(weights, axis=-1), summed)
    denominator = jnp.transpose(totals, (0, 3, 1, 2))[..., None]
    mixed_out = summed / denominator
    mixed_low = mixed_out.astype(jnp.bfloat16).reshape(token_count, query_width)
    attn_out = jnp.einsum("th,dh->td", mixed_low, proj_full, preferred_element_type=jnp.float32)
    hidden_one = flat_tokens + rmsnorm(attn_out, gain_second)
    mid_low = rmsnorm(hidden_one, gain_third).astype(jnp.bfloat16)
    mid_row = lax.all_gather(mid_low.reshape(rows_here, seq_block, D), "seq", axis=1, tiled=True)
    gate_pre = jnp.einsum("btd,df->btf", mid_row, gate_cols, preferred_element_type=jnp.float32)
    up_pre = jnp.einsum("btd,df->btf", mid_row, up_cols, preferred_element_type=jnp.float32)
    activated = gelu_product(gate_pre, up_pre).astype(jnp.bfloat16)
    ffn_terms = jnp.einsum("btf,df->btd", activated, down_cols, preferred_element_type=jnp.float32)
    ffn_out = lax.psum_scatter(ffn_terms, "seq", scatter_dimension=1, tiled=True).reshape(
        token_count, D
    )
    result = hidden_one + rmsnorm(ffn_out, gain_fourth)
    layer_out = result.astype(jnp.bfloat16).reshape(rows_here, seq_block, D)
    upstream = cotangent.astype(jnp.float32).reshape(token_count, D)
    grad_ffn, fourth_part = jax.vjp(rmsnorm, ffn_out, gain_fourth)[1](upstream)
    grad_ffn_low = grad_ffn.astype(jnp.bfloat16)
    grad_row = lax.all_gather(
        grad_ffn_low.reshape(rows_here, seq_block, D), "seq", axis=1, tiled=True
    )
    grad_act = jnp.einsum("btd,df->btf", grad_row, down_cols, preferred_element_type=jnp.float32)
    grad_gate_pre, grad_up_pre = jax.vjp(gelu_product, gate_pre, up_pre)[1](grad_act)
    grad_gate_low = grad_gate_pre.astype(jnp.bfloat16)
    grad_up_low = grad_up_pre.astype(jnp.bfloat16)
    mid_terms = jnp.einsum(
        "btf,df->btd", grad_gate_low, gate_cols, preferred_element_type=jnp.float32
    ) + jnp.einsum("btf,df->btd", grad_up_low, up_cols, preferred_element_type=jnp.float32)
    grad_mid = lax.psum_scatter(mid_terms, "seq", scatter_dimension=1, tiled=True).reshape(
        token_count, D
    )
    column_terms = jnp.stack(
        [
            jnp.einsum("btd,btf->df", mid_row, grad_gate_low, preferred_element_type=jnp.float32),
            jnp.einsum("btd,btf->df", mid_row, grad_up_low, preferred_element_type=jnp.float32),
            jnp.einsum("btd,btf->df", grad_row, activated, preferred_element_type=jnp.float32),
        ]
    )
    returned = lax.all_to_all(
        column_terms.reshape(3, D, 1, col_width).astype(jnp.bfloat16),
        ("rows", "seq"),
        split_axis=1,
        concat_axis=2,
        tiled=True,
    ).astype(jnp.float32)
    column_sums = jnp.sum(
        returned.reshape(3, local_rows, row_groups, seq_count, col_width), axis=2
    ).reshape(3, local_rows, FF)
    hidden_part, third_part = jax.vjp(rmsnorm, hidden_one, gain_third)[1](grad_mid)
    grad_hidden = upstream + hidden_part
    grad_attn, second_part = jax.vjp(rmsnorm, attn_out, gain_second)[1](grad_hidden)
    grad_attn_low = grad_attn.astype(jnp.bfloat16)
    query_back, key_back, value_back, proj_back = (
        lax.all_gather(query_local, ("rows", "seq"), axis=0, tiled=True),
        lax.all_gather(key_local, ("rows", "seq"), axis=0, tiled=True),
        lax.all_gather(value_local, ("rows", "seq"), axis=0, tiled=True),
        lax.all_gather(proj_local, ("rows", "seq"), axis=0, tiled=True),
    )
    grad_mixed = jnp.dot(grad_attn_low, proj_back, preferred_element_type=jnp.float32).reshape(
        rows_here, seq_block, KV_HEADS, group_size, HEAD_DIM
    )
    grad_summed = (grad_mixed / denominator).astype(jnp.bfloat16)
    delta_rows = jnp.transpose(
        jnp.sum(grad_mixed * mixed_out, axis=-1) / denominator[..., 0], (0, 2, 3, 1)
    )
    key_piece = lax.all_gather(key_rot, "seq", axis=1, tiled=True)
    value_piece = lax.all_gather(value_low, "seq", axis=1, tiled=True)
    key_count = key_piece.shape[1]
    weights, bent_score = piece_weights(key_piece)
    grad_weights = (
        jnp.einsum(
            "bqgrd,bkgd->bgrqk", grad_summed, value_piece, preferred_element_type=jnp.float32
        )
        - delta_rows[..., None]
    )
    grad_raw = (weights * grad_weights * (1.0 - bent_score * bent_score)).astype(jnp.bfloat16)
    grad_queries = (
        jnp.einsum("bgrqk,bkgd->bqgrd", grad_raw, key_piece, preferred_element_type=jnp.float32)
        * score_scale
    )
    key_term = (
        jnp.einsum("bgrqk,bqgrd->bkgd", grad_raw, query_rot, preferred_element_type=jnp.float32)
        * score_scale
    )
    value_term = jnp.einsum(
        "bgrqk,bqgrd->bkgd",
        weights.astype(jnp.bfloat16),
        grad_summed,
        preferred_element_type=jnp.float32,
    )
    key_sums = key_term
    value_sums = value_term
    grad_query_rot, key_sums, value_sums = (grad_queries, key_sums, value_sums)
    grad_key_rot, grad_value_sum = (
        lax.psum_scatter(key_sums, "seq", scatter_dimension=1, tiled=True),
        lax.psum_scatter(value_sums, "seq", scatter_dimension=1, tiled=True),
    )
    grad_query_pre = (
        rotate(grad_query_rot.reshape(rows_here, seq_block, HEADS, HEAD_DIM), positions, -1.0)
        .astype(jnp.bfloat16)
        .reshape(token_count, query_width)
    )
    grad_key_pre = (
        rotate(grad_key_rot, positions, -1.0).astype(jnp.bfloat16).reshape(token_count, key_width)
    )
    grad_value_low = grad_value_sum.astype(jnp.bfloat16).reshape(token_count, key_width)
    grad_in = (
        jnp.einsum("tf,df->td", grad_query_pre, query_back, preferred_element_type=jnp.float32)
        + jnp.einsum("tf,df->td", grad_key_pre, key_back, preferred_element_type=jnp.float32)
        + jnp.einsum("tf,df->td", grad_value_low, value_back, preferred_element_type=jnp.float32)
    )
    tokens_part, first_part = jax.vjp(rmsnorm, flat_tokens, gain_first)[1](grad_in)
    grad_tokens = (grad_hidden + tokens_part).reshape(rows_here, seq_block, D)

    def outer_sum(left_side, right_side):
        return jnp.einsum("td,tf->df", left_side, right_side, preferred_element_type=jnp.float32)

    gain_terms = jnp.stack([first_part, second_part, third_part, fourth_part], axis=1)
    padding = jnp.zeros((D, 124), jnp.float32)
    weight_terms = jnp.concatenate(
        [
            outer_sum(normed_low, grad_query_pre),
            outer_sum(normed_low, grad_key_pre),
            outer_sum(normed_low, grad_value_low),
            outer_sum(grad_attn_low, mixed_low),
            gain_terms,
            padding,
        ],
        axis=1,
    )
    summed_terms = lax.psum_scatter(weight_terms, ("rows", "seq"), scatter_dimension=0, tiled=True)
    widths = [query_width, key_width, key_width, query_width]
    pieces_out = []
    column = 0
    for span_cols in widths:
        pieces_out.append(summed_terms[:, column : column + span_cols])
        column = column + span_cols
    return (
        layer_out,
        grad_tokens,
        pieces_out[0],
        pieces_out[1],
        pieces_out[2],
        pieces_out[3],
        column_sums[0],
        column_sums[1],
        column_sums[2],
        summed_terms[:, column],
        summed_terms[:, column + 1],
        summed_terms[:, column + 2],
        summed_terms[:, column + 3],
    )


def solution(mesh):
    placed = (
        P("rows", "seq", None),
        P("rows", "seq", None),
        P("rows", None),
        P(),
        P(("rows", "seq"), None),
        P(("rows", "seq"), None),
        P(("rows", "seq"), None),
        P(("rows", "seq"), None),
        P(("rows", "seq"), None),
        P(("rows", "seq"), None),
        P(("rows", "seq"), None),
        P(),
        P(),
        P(),
        P(),
    )
    return jax.shard_map(
        per_device,
        mesh=mesh,
        in_specs=placed,
        out_specs=(
            P("rows", "seq", None),
            P("rows", "seq", None),
            P(("rows", "seq"), None),
            P(("rows", "seq"), None),
            P(("rows", "seq"), None),
            P(("rows", "seq"), None),
            P(("rows", "seq"), None),
            P(("rows", "seq"), None),
            P(("rows", "seq"), None),
            P(("rows", "seq")),
            P(("rows", "seq")),
            P(("rows", "seq")),
            P(("rows", "seq")),
        ),
        check_vma=False,
    )
```

profile of v0, /device:TPU:0, one launch (start us, length us, event | category | flops | bytes accessed | tf_op | source)
XLA Modules:
  0.0 2727.7 jit_solution(16148281413889453011)
XLA Ops:
  32.4 48.7 %all-gather.14.cloned.1.call-done = bf16[2304,1024]{1,0:T(8,128)(2,1)} async-done(((bf16[72,1024]{1,0:T(8,128)(2,1)}), bf16[2304,1024]{1,0:T(8,128)(2,1)}) %all-gather.14.cloned.1.call-update) | async-done | bytes 4718608 | tf_op jit(solution)/shard_map/all_gather | solution.py:85
  92.8 54.2 %all-gather.10.cloned.1.call-done = bf16[2304,1024]{1,0:T(8,128)(2,1)} async-done(((bf16[72,1024]{1,0:T(8,128)(2,1)}), bf16[2304,1024]{1,0:T(8,128)(2,1)}) %all-gather.10.cloned.1.call-update) | async-done | bytes 4718608 | tf_op jit(solution)/shard_map/all_gather | solution.py:86
  166.9 27.3 %fusion.38 = bf16[72,9216]{1,0:T(8,128)(2,1)} fusion(s32[72,9216]{1,0:T(8,128)S(1)} %copy-done.13, s32[]{:T(128)S(6)} %select_n.149, s32[]{:T(128)} %bitcast.33, s32[]{:T(128)S(6)} %sign.73), kind=kLoop, calls=%fused_computation.56 | loop fusion | flops 8626176 | bytes 3981324 | tf_op jit(solution)/shard_map/convert_element_type | solution.py:80
  194.2 27.7 %fusion.48 = bf16[72,9216]{1,0:T(8,128)(2,1)} fusion(s32[72,9216]{1,0:T(8,128)S(1)} %copy-done.14, s32[]{:T(128)S(6)} %select_n.159, s32[]{:T(128)} %bitcast.35, s32[]{:T(128)S(6)} %sign.77), kind=kLoop, calls=%fused_computation.66 | loop fusion | flops 8626176 | bytes 3981324 | tf_op jit(solution)/shard_map/convert_element_type | solution.py:82
  231.2 12.8 copy.124
  251.2 32.2 %all-gather.16.cloned.1.call-done = bf16[1,2048,4,256]{3,1,2,0:T(8,128)(2,1)} async-done(((bf16[1,128,4,256]{3,1,2,0:T(8,128)(2,1)}), bf16[1,2048,4,256]{3,1,2,0:T(8,128)(2,1)}) %all-gather.16.cloned.1.call-update) | async-done | bytes 4194320 | tf_op jit(solution)/shard_map/all_gather | solution.py:136
  290.4 47.3 %all-gather.12.cloned.1.call-done = bf16[1,2048,4,256]{1,3,2,0:T(8,128)(2,1)} async-done(((bf16[1,128,4,256]{1,3,2,0:T(8,128)(2,1)}), bf16[1,2048,4,256]{1,3,2,0:T(8,128)(2,1)}) %all-gather.12.cloned.1.call-update) | async-done | bytes 4194320 | tf_op jit(solution)/shard_map/all_gather | solution.py:137
  346.1 75.1 %all-gather.20.cloned.1.call-done = bf16[2304,2048]{1,0:T(8,128)(2,1)} async-done(((bf16[72,2048]{1,0:T(8,128)(2,1)}), bf16[2304,2048]{1,0:T(8,128)(2,1)}) %all-gather.20.cloned.1.call-update) | async-done | bytes 9437200 | tf_op jit(solution)/shard_map/all_gather | solution.py:87
  429.7 29.0 %fusion.43 = bf16[72,9216]{1,0:T(8,128)(2,1)} fusion(s32[72,9216]{1,0:T(8,128)} %param.24, s32[]{:T(128)S(6)} %select_n.154, s32[]{:T(128)} %bitcast.34, s32[]{:T(128)S(6)} %sign.75), kind=kLoop, calls=%fused_computation.61 | loop fusion | flops 8626176 | bytes 3981324 | tf_op jit(solution)/shard_map/convert_element_type | solution.py:81
  489.3 209.2 %all_to_all.24 = bf16[3,72,32,576]{3,1,0,2:T(8,128)(2,1)S(1)} all-to-all(bf16[3,72,32,576]{3,1,0,2:T(8,128)(2,1)} %copy.126), channel_id=1, replica_groups=mesh['rows'=2,'seq'=16] {'rows','seq'}, dimensions={2} | all-to-all | bytes 15925248 | tf_op jit(solution)/shard_map/all_to_all | solution.py:96
  711.6 12.6 multiply_convert_fusion.1
  737.2 191.9 %reduce-scatter.6.cloned.1.call-done = f32[1,128,2304]{2,1,0:T(8,128)} async-done(((f32[1,2048,2304]{2,1,0:T(8,128)}), f32[1,128,2304]{2,1,0:T(8,128)}) %reduce-scatter.6.cloned.1.call-update) | async-done | bytes 1179664 | tf_op jit(solution)/shard_map/reduce_scatter | solution.py:157
  934.7 80.7 %all-gather.22.cloned.1.call-done = bf16[1,2048,2304]{2,1,0:T(8,128)(2,1)} async-done(((bf16[1,128,2304]{2,1,0:T(8,128)(2,1)}), bf16[1,2048,2304]{2,1,0:T(8,128)(2,1)}) %all-gather.22.cloned.1.call-update) | async-done | bytes 9437200 | tf_op jit(solution)/shard_map/all_gather | solution.py:165
  1015.3 16.0 multiply_convert_fusion
  1042.2 19.0 add_bitcast_fusion
  1061.3 193.2 %reduce-scatter.8.cloned.1.call-done = f32[1,128,2304]{2,1,0:T(8,128)} async-done(((f32[1,2048,2304]{2,1,0:T(8,128)}), f32[1,128,2304]{2,1,0:T(8,128)}) %reduce-scatter.8.cloned.1.call-update) | async-done | bytes 1179664 | tf_op jit(solution)/shard_map/reduce_scatter | solution.py:175
  1321.3 61.2 %reduce-scatter.10.cloned.1.call-done = f32[1,128,4,256]{3,1,2,0:T(8,128)} async-done(((f32[1,2048,4,256]{3,1,2,0:T(8,128)}), f32[1,128,4,256]{3,1,2,0:T(8,128)}) %reduce-scatter.10.cloned.1.call-update) | async-done | bytes 524304 | tf_op jit(solution)/shard_map/reduce_scatter | solution.py:241
  1383.8 107.2 %reduce-scatter.12.cloned.1.call-done = f32[1,128,4,256]{1,3,2,0:T(8,128)} async-done(((f32[1,2048,4,256]{1,3,2,0:T(8,128)}), f32[1,128,4,256]{1,3,2,0:T(8,128)}) %reduce-scatter.12.cloned.1.call-update) | async-done | bytes 524304 | tf_op jit(solution)/shard_map/reduce_scatter | solution.py:242
  1508.1 132.7 %concatenate.69 = f32[2304,6272]{0,1:T(8,128)} concatenate(f32[2304,2048]{0,1:T(8,128)} %fusion.111, f32[2304,1024]{0,1:T(8,128)} %fusion.113, f32[2304,1024]{0,1:T(8,128)} %fusion.109, f32[2304,2048]{0,1:T(8,128)} %fusion.158, f32[2304,1]{0,1:T(1,128)S(1)} %stack.40, f32[2304,1]{0,1:T(1,128)S(1)} %copy-done.29, f32[2304,1]{0,1:T(1,128)S(1)} %copy-done.28, ...), dimensions={1} | concatenate | bytes 115605504 | tf_op jit(solution)/shard_map/concatenate | solution.py:266
  1672.2 19.6 copy.140
  1696.3 380.9 %all-to-all-done.1 = bf16[3,2304,1,576]{3,0,2,1:T(4,128)(2,1)} async-done(((bf16[3,2304,1,576]{3,0,2,1:T(4,128)(2,1)}), bf16[3,2304,1,576]{3,0,2,1:T(4,128)(2,1)}, u32[]{:S(2)}, u32[]{:S(2)}) %all-to-all-start.1) | async-done | bytes 7962656 | tf_op jit(solution)/shard_map/all_to_all | solution.py:185
  2086.7 11.0 convert.36
  2097.7 12.1 reduce_sum.170
  2137.5 573.2 %all-reduce.3.cloned.1.call-done = f32[2304,6272]{0,1:T(8,128)} async-done(((f32[2304,6272]{0,1:T(8,128)}), f32[2304,6272]{0,1:T(8,128)}) %all-reduce.3.cloned.1.call-update) | async-done | bytes 57802768
  (239 shorter events, 328.9 us)
Async XLA Ops:
  7.2 73.9 %all-gather.14.cloned.1.call-start = ((), (), s32[]{:S(2)}) async-start(), calls=%async_computation.8 | async-start | bytes 4866048 | tf_op jit(solution)/shard_map/all_gather | solution.py:85
  14.6 132.3 %all-gather.10.cloned.1.call-start = ((), (), s32[]{:S(2)}) async-start(), calls=%async_computation.6 | async-start | bytes 4866048 | tf_op jit(solution)/shard_map/all_gather | solution.py:86
  20.6 210.7 %all-gather.18.cloned.1.call-start = ((), (), s32[]{:S(2)}) async-start(), calls=%async_computation.10 | async-start | bytes 9732096 | tf_op jit(solution)/shard_map/all_gather | solution.py:84
  30.1 253.3 %all-gather.16.cloned.1.call-start = ((), (), s32[]{:S(2)}) async-start(), calls=%async_computation.9 | async-start | bytes 4456448 | tf_op jit(solution)/shard_map/all_gather | solution.py:136
  31.4 56.4 %copy-start.38 = (f32[128]{0:T(128)}, f32[128]{0:T(128)S(1)}, u32[]{:S(2)}) copy-start(f32[128]{0:T(128)S(1)} %fusion.77) | copy-start | bytes 1540
  31.4 212.6 %copy-start.30 = (f32[128]{0:T(128)}, f32[128]{0:T(128)S(1)}, u32[]{:S(2)}) copy-start(f32[128]{0:T(128)S(1)} %fusion.132) | copy-start | bytes 1540
  31.4 212.6 %copy-start.22 = (f32[2304]{0:T(1024)}, f32[2304]{0:T(1024)S(1)}, u32[]{:S(2)}) copy-start(f32[2304]{0:T(1024)S(1)} %broadcast_add_fusion.3) | copy-start | bytes 27652
  32.4 218.6 %copy-start.17 = (f32[128,128]{1,0:T(8,128)}, f32[128,128]{1,0:T(8,128)S(1)}, u32[]{:S(2)}) copy-start(f32[128,128]{1,0:T(8,128)S(1)} %get-tuple-element.116) | copy-start | bytes 196612
  92.7 73.1 %copy-start.36 = (s32[1,2048]{1,0:T(1,128)S(1)}, s32[1,2048]{1,0:T(1,128)}, u32[]{:S(2)}) copy-start(s32[1,2048]{1,0:T(1,128)} %param.17) | copy-start | bytes 24580
  92.7 73.1 %copy-start.33 = (f32[2304]{0:T(1024)S(1)}, f32[2304]{0:T(1024)}, u32[]{:S(2)}) copy-start(f32[2304]{0:T(1024)} %param.27) | copy-start | bytes 27652
  92.7 73.2 %copy-start.34 = (f32[2304]{0:T(1024)S(1)}, f32[2304]{0:T(1024)}, u32[]{:S(2)}) copy-start(f32[2304]{0:T(1024)} %param.28) | copy-start | bytes 27652
  92.7 74.2 %copy-start.13 = (s32[72,9216]{1,0:T(8,128)S(1)}, s32[72,9216]{1,0:T(8,128)}, u32[]{:S(2)}) copy-start(s32[72,9216]{1,0:T(8,128)} %param.23) | copy-start | bytes 7962628
  92.7 245.0 %all-gather.12.cloned.1.call-start = ((), (), s32[]{:S(2)}) async-start(), calls=%async_computation.7 | async-start | bytes 4456448 | tf_op jit(solution)/shard_map/all_gather | solution.py:137
  152.6 268.6 %all-gather.20.cloned.1.call-start = ((), (), s32[]{:S(2)}) async-start(), calls=%async_computation.11 | async-start | bytes 9732096 | tf_op jit(solution)/shard_map/all_gather | solution.py:87
  161.8 540.3 %all-gather.24.cloned.1.call-start = ((), (), s32[]{:S(2)}) async-start(), calls=%async_computation.17 | async-start | bytes 10027008 | tf_op jit(solution)/shard_map/all_gather | solution.py:152
  346.1 82.1 %copy-start.15 = (bf16[1,128,4,2,256]{1,4,3,2,0:T(8,128)(2,1)}, bf16[1,128,4,2,256]{1,4,3,2,0:T(8,128)(2,1)S(1)}, u32[]{:S(2)}) copy-start(bf16[1,128,4,2,256]{1,4,3,2,0:T(8,128)(2,1)S(1)} %get-tuple-element.126) | copy-start | bytes 1572868
  429.6 499.5 %reduce-scatter.6.cloned.1.call-start = ((), (), s32[]{:S(2)}) async-start(), calls=%async_computation.12 | async-start | bytes 20054016 | tf_op jit(solution)/shard_map/reduce_scatter | solution.py:157
  736.5 194.1 %copy-start.6 = (bf16[1,128,2304]{2,1,0:T(8,128)(2,1)S(1)}, bf16[1,128,2304]{2,1,0:T(8,128)(2,1)}, u32[]{:S(2)}) copy-start(bf16[1,128,2304]{2,1,0:T(8,128)(2,1)} %param.16) | copy-start | bytes 1769476
  736.5 278.8 %all-gather.22.cloned.1.call-start = ((), (), s32[]{:S(2)}) async-start(), calls=%async_computation.13 | async-start | bytes 10027008 | tf_op jit(solution)/shard_map/all_gather | solution.py:165
  934.6 319.8 %reduce-scatter.8.cloned.1.call-start = ((), (), s32[]{:S(2)}) async-start(), calls=%async_computation.14 | async-start | bytes 20054016 | tf_op jit(solution)/shard_map/reduce_scatter | solution.py:175
  1061.2 321.2 %reduce-scatter.10.cloned.1.call-start = ((), (), s32[]{:S(2)}) async-start(), calls=%async_computation.15 | async-start | bytes 8912896 | tf_op jit(solution)/shard_map/reduce_scatter | solution.py:241
  1278.5 212.5 %reduce-scatter.12.cloned.1.call-start = ((), (), s32[]{:S(2)}) async-start(), calls=%async_computation.16 | async-start | bytes 8912896 | tf_op jit(solution)/shard_map/reduce_scatter | solution.py:242
  1288.5 1422.2 %all-reduce.3.cloned.1.call-start = ((), (), s32[]{:S(2)}) async-start(), calls=%async_computation.18 | async-start | bytes 115605504
  1691.8 385.4 %all-to-all-start.1 = ((bf16[3,2304,1,576]{3,0,2,1:T(4,128)(2,1)}), bf16[3,2304,1,576]{3,0,2,1:T(4,128)(2,1)}, u32[]{:S(2)}, u32[]{:S(2)}) async-start(bf16[3,2304,1,576]{3,0,2,1:T(4,128)(2,1)} %copy.140), calls=%async_computation.5 | async-start | bytes 23592960 | tf_op jit(solution)/shard_map/all_to_all | solution.py:185
  (44 other events, 431.5 us)
Sparse Core Ops, SparseCore 0:
  14.8 66.2 all-gather.13
  84.5 62.3 all-gather.9
  150.4 80.7 all-gather.17
  233.9 49.4 all-gather.15
  285.9 51.6 all-gather.11
  341.0 80.1 all-gather.19
  429.7 95.4 all-gather.23
  736.6 192.4 reduce-scatter.5
  934.7 80.5 all-gather.21
  1061.4 193.0 reduce-scatter.7
  1278.6 103.8 reduce-scatter.9
  1386.4 104.5 reduce-scatter.11
  1641.0 1069.6 all-reduce.2
where the time goes:
time: 2740 us; the launch traced here: 2730 us
  waiting for transfers between devices  1860 us (68%)
  local copies, waits for them, and re-layouts  255 us (9%)
  matrix products  216 us (8%)
  blocking collectives  209 us (8%)
  other arithmetic  163 us (6%)
    unnamed x14, waiting for transfers between devices  573 us
    all_to_all x1, waiting for transfers between devices, per_device(): lax.all_to_all(column_terms.reshape(3, D, 1, col_width).astype(jnp.bfloat...  381 us
    all_to_all x1, blocking collectives, per_device(): lax.all_to_all(spread, ('rows', 'seq'), split_axis=2, concat_axis=1, tile...  209 us
    reduce_scatter x1, waiting for transfers between devices, per_device(): lax.psum_scatter(mid_terms, 'seq', scatter_dimension=1, tiled=True)  193 us
    reduce_scatter x1, waiting for transfers between devices, per_device(): lax.psum_scatter(ffn_terms, 'seq', scatter_dimension=1, tiled=True)  192 us
    concatenate x1, local copies, waits for them, and re-layouts, per_device(): jnp.concatenate([outer_sum(normed_low, grad_query_pre), outer_sum(normed_...  133 us
    reduce_scatter x1, waiting for transfers between devices, per_device(): lax.psum_scatter(value_sums, 'seq', scatter_dimension=1, tiled=True)  107 us
    all_gather x1, waiting for transfers between devices, per_device(): lax.all_gather(grad_ffn_low.reshape(rows_here, seq_block, D), 'seq', axis...  80.7 us
  transfers between devices with their start and end apart: 14, of which 13 were waited for; matrix products, arithmetic and copies ran while one was open for 13% of the time, Pallas kernels for 0%

commit v1 on v0

--- a/solution.py
+++ b/solution.py
@@ -133,8 +133,13 @@
         weights = jnp.where(allowed[:, None, None], jnp.exp(softcap * bent_score), 0.0)
         return (weights, bent_score)
 
-    key_piece = lax.all_gather(key_rot, "seq", axis=1, tiled=True)
-    value_piece = lax.all_gather(value_low, "seq", axis=1, tiled=True)
+    key_piece, value_piece = jnp.split(
+        lax.all_gather(
+            jnp.concatenate([key_rot, value_low], axis=0), axis_name="seq", axis=1, tiled=True
+        ),
+        [key_rot.shape[0]],
+        axis=0,
+    )
     weights, bent_score = piece_weights(key_piece)
     summed = jnp.einsum(
         "bgrqk,bkgd->bqgrd",

time: 2740 us -> 2760 us (level)
    all_gather x0 -> x1, waiting for transfers between devices: none -> 56.3 us  [per_device(): lax.all_gather(jnp.concatenate([key_rot, value_low], axis=0), axis_name='...]
    all_gather x1, waiting for transfers between devices: 32.2 us -> 4.29 us  [per_device(): key_piece = lax.all_gather(key_rot, 'seq', axis=1, tiled=True)]
    unnamed x14 -> x15, waiting for transfers between devices: 573 us -> 574 us
  transfers between devices with their start and end apart: 14 -> 15, of which waited for: 13 -> 14; matrix products, arithmetic and copies ran while one was open for 13% -> 15% of each run, Pallas kernels for 0% -> 0%
where the time goes in v1:
time: 2760 us; the launch traced here: 2750 us
  waiting for transfers between devices  1880 us (68%)
  local copies, waits for them, and re-layouts  254 us (9%)
  matrix products  215 us (8%)
  blocking collectives  209 us (8%)
  other arithmetic  164 us (6%)
    unnamed x15, waiting for transfers between devices  574 us
    all_to_all x1, waiting for transfers between devices, per_device(): lax.all_to_all(column_terms.reshape(3, D, 1, col_width).astype(jnp.bfloat...  381 us
    all_to_all x1, blocking collectives, per_device(): lax.all_to_all(spread, ('rows', 'seq'), split_axis=2, concat_axis=1, tile...  209 us
    reduce_scatter x1, waiting for transfers between devices, per_device(): lax.psum_scatter(ffn_terms, 'seq', scatter_dimension=1, tiled=True)  192 us
    reduce_scatter x1, waiting for transfers between devices, per_device(): lax.psum_scatter(mid_terms, 'seq', scatter_dimension=1, tiled=True)  191 us
    concatenate x1, local copies, waits for them, and re-layouts, per_device(): jnp.concatenate([outer_sum(normed_low, grad_query_pre), outer_sum(normed_...  133 us
    reduce_scatter x1, waiting for transfers between devices, per_device(): lax.psum_scatter(value_sums, 'seq', scatter_dimension=1, tiled=True)  107 us
    all_gather x1, waiting for transfers between devices, per_device(): lax.all_gather(grad_ffn_low.reshape(rows_here, seq_block, D), 'seq', axis...  78.9 us
  transfers between devices with their start and end apart: 15, of which 14 were waited for; matrix products, arithmetic and copies ran while one was open for 15% of the time, Pallas kernels for 0%

profile of v1, /device:TPU:0, one launch (start us, length us, event | category | flops | bytes accessed | tf_op | source)
XLA Modules:
  0.0 2748.9 jit_solution(3117528931341905655)
XLA Ops:
  32.5 48.6 %all-gather.13.cloned.1.call-done = bf16[2304,1024]{1,0:T(8,128)(2,1)} async-done(((bf16[72,1024]{1,0:T(8,128)(2,1)}), bf16[2304,1024]{1,0:T(8,128)(2,1)}) %all-gather.13.cloned.1.call-update) | async-done | bytes 4718608 | tf_op jit(solution)/shard_map/all_gather | solution.py:86
  84.6 62.4 %all-gather.11.cloned.1.call-done = bf16[2304,1024]{1,0:T(8,128)(2,1)} async-done(((bf16[72,1024]{1,0:T(8,128)(2,1)}), bf16[2304,1024]{1,0:T(8,128)(2,1)}) %all-gather.11.cloned.1.call-update) | async-done | bytes 4718608 | tf_op jit(solution)/shard_map/all_gather | solution.py:85
  173.7 27.3 fusion.50
  201.0 27.6 %fusion.60 = bf16[72,9216]{1,0:T(8,128)(2,1)} fusion(s32[72,9216]{1,0:T(8,128)S(1)} %copy-done.14, s32[]{:T(128)S(6)} %select_n.161, s32[]{:T(128)} %bitcast.34, s32[]{:T(128)S(6)} %sign.77), kind=kLoop, calls=%fused_computation.79 | loop fusion | flops 8626176 | bytes 3981324 | tf_op jit(solution)/shard_map/convert_element_type | solution.py:82
  231.5 12.7 copy.130
  251.4 56.3 %all-gather.15.cloned.1.call-done = bf16[2,2048,4,256]{3,1,2,0:T(8,128)(2,1)} async-done(((bf16[2,128,4,256]{3,1,2,0:T(8,128)(2,1)}), bf16[2,2048,4,256]{3,1,2,0:T(8,128)(2,1)}) %all-gather.15.cloned.1.call-update) | async-done | bytes 8388624 | tf_op jit(solution)/shard_map/all_gather | solution.py:137
  316.3 75.0 %all-gather.19.cloned.1.call-done = bf16[2304,2048]{1,0:T(8,128)(2,1)} async-done(((bf16[72,2048]{1,0:T(8,128)(2,1)}), bf16[2304,2048]{1,0:T(8,128)(2,1)}) %all-gather.19.cloned.1.call-update) | async-done | bytes 9437200 | tf_op jit(solution)/shard_map/all_gather | solution.py:87
  399.7 29.0 %fusion.55 = bf16[72,9216]{1,0:T(8,128)(2,1)} fusion(s32[72,9216]{1,0:T(8,128)} %param.24, s32[]{:T(128)S(6)} %select_n.156, s32[]{:T(128)} %bitcast.33, s32[]{:T(128)S(6)} %sign.75), kind=kLoop, calls=%fused_computation.74 | loop fusion | flops 8626176 | bytes 3981324 | tf_op jit(solution)/shard_map/convert_element_type | solution.py:81
  459.3 209.3 %all_to_all.24 = bf16[3,72,32,576]{3,1,0,2:T(8,128)(2,1)S(1)} all-to-all(bf16[3,72,32,576]{3,1,0,2:T(8,128)(2,1)} %copy.133), channel_id=1, replica_groups=mesh['rows'=2,'seq'=16] {'rows','seq'}, dimensions={2} | all-to-all | bytes 15925248 | tf_op jit(solution)/shard_map/all_to_all | solution.py:96
  681.5 12.7 multiply_convert_fusion.1
  707.2 191.9 %reduce-scatter.6.cloned.1.call-done = f32[1,128,2304]{2,1,0:T(8,128)} async-done(((f32[1,2048,2304]{2,1,0:T(8,128)}), f32[1,128,2304]{2,1,0:T(8,128)}) %reduce-scatter.6.cloned.1.call-update) | async-done | bytes 1179664 | tf_op jit(solution)/shard_map/reduce_scatter | solution.py:162
  906.5 78.9 %all-gather.21.cloned.1.call-done = bf16[1,2048,2304]{2,1,0:T(8,128)(2,1)} async-done(((bf16[1,128,2304]{2,1,0:T(8,128)(2,1)}), bf16[1,2048,2304]{2,1,0:T(8,128)(2,1)}) %all-gather.21.cloned.1.call-update) | async-done | bytes 9437200 | tf_op jit(solution)/shard_map/all_gather | solution.py:170
  985.3 16.0 multiply_convert_fusion
  1012.1 19.5 add_bitcast_fusion
  1043.6 190.7 %reduce-scatter.8.cloned.1.call-done = f32[1,128,2304]{2,1,0:T(8,128)} async-done(((f32[1,2048,2304]{2,1,0:T(8,128)}), f32[1,128,2304]{2,1,0:T(8,128)}) %reduce-scatter.8.cloned.1.call-update) | async-done | bytes 1179664 | tf_op jit(solution)/shard_map/reduce_scatter | solution.py:180
  1244.5 41.7 %all-gather.25.cloned.1.call-done = bf16[1,2048,4,256]{3,1,2,0:T(8,128)(2,1)} async-done(((bf16[1,128,4,256]{3,1,2,0:T(8,128)(2,1)}), bf16[1,2048,4,256]{3,1,2,0:T(8,128)(2,1)}) %all-gather.25.cloned.1.call-update) | async-done | bytes 4194320 | tf_op jit(solution)/shard_map/all_gather | solution.py:218
  1342.9 60.7 %reduce-scatter.10.cloned.1.call-done = f32[1,128,4,256]{3,1,2,0:T(8,128)} async-done(((f32[1,2048,4,256]{3,1,2,0:T(8,128)}), f32[1,128,4,256]{3,1,2,0:T(8,128)}) %reduce-scatter.10.cloned.1.call-update) | async-done | bytes 524304 | tf_op jit(solution)/shard_map/reduce_scatter | solution.py:246
  1404.9 107.4 %reduce-scatter.12.cloned.1.call-done = f32[1,128,4,256]{1,3,2,0:T(8,128)} async-done(((f32[1,2048,4,256]{1,3,2,0:T(8,128)}), f32[1,128,4,256]{1,3,2,0:T(8,128)}) %reduce-scatter.12.cloned.1.call-update) | async-done | bytes 524304 | tf_op jit(solution)/shard_map/reduce_scatter | solution.py:247
  1529.4 132.7 %concatenate.74 = f32[2304,6272]{0,1:T(8,128)} concatenate(f32[2304,2048]{0,1:T(8,128)} %fusion.123, f32[2304,1024]{0,1:T(8,128)} %fusion.125, f32[2304,1024]{0,1:T(8,128)} %fusion.121, f32[2304,2048]{0,1:T(8,128)} %fusion.175, f32[2304,1]{0,1:T(1,128)S(1)} %stack.40, f32[2304,1]{0,1:T(1,128)S(1)} %copy-done.33, f32[2304,1]{0,1:T(1,128)S(1)} %copy-done.32, ...), dimensions={1} | concatenate | bytes 115605504 | tf_op jit(solution)/shard_map/concatenate | solution.py:271
  1693.5 19.6 copy.147
  1717.5 380.9 %all-to-all-done.1 = bf16[3,2304,1,576]{3,0,2,1:T(4,128)(2,1)} async-done(((bf16[3,2304,1,576]{3,0,2,1:T(4,128)(2,1)}), bf16[3,2304,1,576]{3,0,2,1:T(4,128)(2,1)}, u32[]{:S(2)}, u32[]{:S(2)}) %all-to-all-start.1) | async-done | bytes 7962656 | tf_op jit(solution)/shard_map/all_to_all | solution.py:190
  2107.9 11.0 convert.36
  2118.9 12.2 reduce_sum.170
  2158.7 573.3 %all-reduce.3.cloned.1.call-done = f32[2304,6272]{0,1:T(8,128)} async-done(((f32[2304,6272]{0,1:T(8,128)}), f32[2304,6272]{0,1:T(8,128)}) %all-reduce.3.cloned.1.call-update) | async-done | bytes 57802768
  (253 shorter events, 327.7 us)
Async XLA Ops:
  7.2 73.9 %copy-start = (bf16[1,128,2304]{2,1,0:T(8,128)(2,1)S(1)}, bf16[1,128,2304]{2,1,0:T(8,128)(2,1)}, u32[]{:S(2)}) copy-start(bf16[1,128,2304]{2,1,0:T(8,128)(2,1)} %param.15) | copy-start | bytes 1769476
  7.2 73.9 %all-gather.13.cloned.1.call-start = ((), (), s32[]{:S(2)}) async-start(), calls=%async_computation.7 | async-start | bytes 4866048 | tf_op jit(solution)/shard_map/all_gather | solution.py:86
  14.7 132.3 %all-gather.11.cloned.1.call-start = ((), (), s32[]{:S(2)}) async-start(), calls=%async_computation.6 | async-start | bytes 4866048 | tf_op jit(solution)/shard_map/all_gather | solution.py:85
  20.6 210.9 %all-gather.17.cloned.1.call-start = ((), (), s32[]{:S(2)}) async-start(), calls=%async_computation.9 | async-start | bytes 9732096 | tf_op jit(solution)/shard_map/all_gather | solution.py:84
  30.1 277.6 %all-gather.15.cloned.1.call-start = ((), (), s32[]{:S(2)}) async-start(), calls=%async_computation.8 | async-start | bytes 8912896 | tf_op jit(solution)/shard_map/all_gather | solution.py:137
  31.4 212.8 %copy-start.34 = (f32[128]{0:T(128)}, f32[128]{0:T(128)S(1)}, u32[]{:S(2)}) copy-start(f32[128]{0:T(128)S(1)} %fusion.144) | copy-start | bytes 1540
  31.5 212.8 %copy-start.24 = (f32[2304]{0:T(1024)}, f32[2304]{0:T(1024)S(1)}, u32[]{:S(2)}) copy-start(f32[2304]{0:T(1024)S(1)} %broadcast_add_fusion.3) | copy-start | bytes 27652
  84.6 73.3 %copy-start.15 = (bf16[1,128,4,256]{3,1,2,0:T(8,128)(2,1)}, bf16[1,128,4,256]{3,1,2,0:T(8,128)(2,1)S(1)}, u32[]{:S(2)}) copy-start(bf16[1,128,4,256]{3,1,2,0:T(8,128)(2,1)S(1)} %copy.129) | copy-start | bytes 786436
  159.5 231.8 %all-gather.19.cloned.1.call-start = ((), (), s32[]{:S(2)}) async-start(), calls=%async_computation.10 | async-start | bytes 9732096 | tf_op jit(solution)/shard_map/all_gather | solution.py:87
  168.6 503.4 %all-gather.27.cloned.1.call-start = ((), (), s32[]{:S(2)}) async-start(), calls=%async_computation.18 | async-start | bytes 10027008 | tf_op jit(solution)/shard_map/all_gather | solution.py:157
  172.6 28.4 %copy-start.14 = (s32[72,9216]{1,0:T(8,128)S(1)}, s32[72,9216]{1,0:T(8,128)}, u32[]{:S(2)}) copy-start(s32[72,9216]{1,0:T(8,128)} %param.25) | copy-start | bytes 7962628
  244.3 63.4 %copy-start.29 = (pred[128,2048]{0,1:T(8,128)(4,1)S(1)}, pred[128,2048]{0,1:T(8,128)(4,1)}, u32[]{:S(2)}) copy-start(pred[128,2048]{0,1:T(8,128)(4,1)} %fusion.103) | copy-start | bytes 786436
  316.3 81.9 %copy-start.16 = (bf16[1,128,4,2,256]{1,4,3,2,0:T(8,128)(2,1)}, bf16[1,128,4,2,256]{1,4,3,2,0:T(8,128)(2,1)S(1)}, u32[]{:S(2)}) copy-start(bf16[1,128,4,2,256]{1,4,3,2,0:T(8,128)(2,1)S(1)} %get-tuple-element.126) | copy-start | bytes 1572868
  399.7 499.4 %reduce-scatter.6.cloned.1.call-start = ((), (), s32[]{:S(2)}) async-start(), calls=%async_computation.11 | async-start | bytes 20054016 | tf_op jit(solution)/shard_map/reduce_scatter | solution.py:162
  706.5 194.2 %copy-start.6 = (bf16[1,128,2304]{2,1,0:T(8,128)(2,1)S(1)}, bf16[1,128,2304]{2,1,0:T(8,128)(2,1)}, u32[]{:S(2)}) copy-start(bf16[1,128,2304]{2,1,0:T(8,128)(2,1)} %param.16) | copy-start | bytes 1769476
  706.5 278.8 %all-gather.21.cloned.1.call-start = ((), (), s32[]{:S(2)}) async-start(), calls=%async_computation.12 | async-start | bytes 10027008 | tf_op jit(solution)/shard_map/all_gather | solution.py:170
  904.6 132.2 %all-gather.23.cloned.1.call-start = ((), (), s32[]{:S(2)}) async-start(), calls=%async_computation.14 | async-start | bytes 4456448 | tf_op jit(solution)/shard_map/all_gather | solution.py:217
  906.4 327.8 %reduce-scatter.8.cloned.1.call-start = ((), (), s32[]{:S(2)}) async-start(), calls=%async_computation.13 | async-start | bytes 20054016 | tf_op jit(solution)/shard_map/reduce_scatter | solution.py:180
  1031.6 254.6 %all-gather.25.cloned.1.call-start = ((), (), s32[]{:S(2)}) async-start(), calls=%async_computation.15 | async-start | bytes 4456448 | tf_op jit(solution)/shard_map/all_gather | solution.py:218
  1032.3 371.3 %reduce-scatter.10.cloned.1.call-start = ((), (), s32[]{:S(2)}) async-start(), calls=%async_computation.16 | async-start | bytes 8912896 | tf_op jit(solution)/shard_map/reduce_scatter | solution.py:246
  1238.0 48.2 %copy-start.30 = (pred[128,2048]{0,1:T(8,128)(4,1)S(1)}, pred[128,2048]{0,1:T(8,128)(4,1)}, u32[]{:S(2)}) copy-start(pred[128,2048]{0,1:T(8,128)(4,1)} %fusion.103) | copy-start | bytes 786436
  1300.4 211.9 %reduce-scatter.12.cloned.1.call-start = ((), (), s32[]{:S(2)}) async-start(), calls=%async_computation.17 | async-start | bytes 8912896 | tf_op jit(solution)/shard_map/reduce_scatter | solution.py:247
  1310.3 1421.6 %all-reduce.3.cloned.1.call-start = ((), (), s32[]{:S(2)}) async-start(), calls=%async_computation.19 | async-start | bytes 115605504
  1713.1 385.2 %all-to-all-start.1 = ((bf16[3,2304,1,576]{3,0,2,1:T(4,128)(2,1)}), bf16[3,2304,1,576]{3,0,2,1:T(4,128)(2,1)}, u32[]{:S(2)}, u32[]{:S(2)}) async-start(bf16[3,2304,1,576]{3,0,2,1:T(4,128)(2,1)} %copy.147), calls=%async_computation.5 | async-start | bytes 23592960 | tf_op jit(solution)/shard_map/all_to_all | solution.py:190
  (49 other events, 384.9 us)
Sparse Core Ops, SparseCore 0:
  14.8 66.2 all-gather.12
  84.5 62.3 all-gather.10
  150.4 81.0 all-gather.16
  234.1 73.4 all-gather.14
  311.0 80.2 all-gather.18
  399.8 95.4 all-gather.26
  706.6 192.4 reduce-scatter.5
  904.8 80.5 all-gather.20
  988.1 48.7 all-gather.22
  1040.8 193.4 reduce-scatter.7
  1236.5 49.6 all-gather.24
  1300.5 103.0 reduce-scatter.9
  1407.7 104.5 reduce-scatter.11
  1662.2 1069.6 all-reduce.2
